TPU v7x, 256 devices: a whole 4x4x8 slice. The times are simulated.
256 devices in a mesh: tm: 8 (over x_hi, y), chan: 32 (over z, x_lo, core).
Axes of the slice: x: 4 (x_hi: 2, x_lo: 2; x = x_hi * 2 + x_lo), y: 4, z: 8, core: 2. Of those that a mesh axis runs over, the one named last changes fastest.
Arguments:
- vis: bfloat16 [512, 1024, 512], P('tm', 'chan'), may hold values from -6 to 6
- beam: bfloat16 [16, 1024, 2, 64, 256], P('tm', 'chan'), may hold values from -0.25 to 0.25
- fg_cov: float32 [1024, 1024], replicated, may hold values from 0 to 30, as said below
- flags: int32 [1024], replicated, may hold values 0 or 1
- m_modes: int32 [16], replicated, may hold values from 0 to 255, as said below
Outputs:
- filled: float32 [16, 2, 64, 1024], P('tm', None, None, 'chan')
Inputs may be any that keep to these rules, and one draw needn't show every extreme that they name: `m_modes`: m numbers of the window; entries may repeat. `fg_cov`: symmetric and positive definite.
All inputs are finite; a program needn't handle non-finite values.
Results may differ from a plain program's by a relative error of at most 0.0085.
Values sent between devices are 32-bit elements; how exact they have to be, the bound alone decides.
A program may use at most 64 MiB of HBM per device.

v0:
```python
import math
import jax
import jax.numpy as jnp
from jax import lax
from jax.sharding import PartitionSpec as P

ITERS = 10
EPS = 1e-06


def conjugate_fill(rows, good, apply_cov, curv_total, norm_total):

    def operator(vec):
        return vec + good * apply_cov(good * vec)

    start = good * rows
    norm_now = norm_total(start * start)[:, None]

    def advance(step, carry):
        sol, resid, direc, norm_now = carry
        image = operator(direc)
        alpha = norm_now / (curv_total(direc * image)[:, None] + EPS)
        sol = sol + alpha * direc
        resid = resid - alpha * image
        norm_next = norm_total(resid * resid)[:, None]
        direc = resid + norm_next / (norm_now + EPS) * direc
        return (sol, resid, direc, norm_next)

    sol, resid, direc, norm_now = lax.fori_loop(
        0, ITERS, advance, (jnp.zeros_like(rows), start, start, norm_now)
    )
    signal = apply_cov(good * sol)
    return good * rows + (1.0 - good) * signal


def per_device(vis, beam, fg_cov, flags, m_modes):
    t_dev = vis.shape[0]
    f_dev = vis.shape[1]
    width = vis.shape[2]
    half_width = width // 2
    n_time = t_dev * lax.axis_size("tm")
    m_dev = m_modes.shape[0] // lax.axis_size("tm")
    times = lax.axis_index("tm") * t_dev + jnp.arange(t_dev, dtype=jnp.int32)
    flat = vis.reshape(t_dev, f_dev * width)
    scale = 1.0 / math.sqrt(n_time)
    index = m_modes[:, None] * times[None, :] % n_time
    angle = 2.0 * math.pi / n_time * index.astype(jnp.float32)
    tables = jnp.concatenate([jnp.cos(angle), jnp.sin(angle)], axis=0).astype(jnp.bfloat16)
    prod = jnp.dot(tables, flat, preferred_element_type=jnp.float32).reshape(
        2, m_dev * lax.axis_size("tm"), f_dev, width
    )
    cos_part = prod[0]
    sin_part = prod[1]
    real_part = (cos_part[..., :half_width] + sin_part[..., half_width:]) * scale
    imag_part = (cos_part[..., half_width:] - sin_part[..., :half_width]) * scale
    mvis = lax.psum_scatter(
        jnp.concatenate([real_part, imag_part], axis=-1), "tm", scatter_dimension=0, tiled=True
    ).astype(jnp.bfloat16)
    prods = jnp.einsum(
        "mfpln,mfqn->mpqlf",
        beam,
        mvis.reshape(m_dev, f_dev, 2, half_width),
        preferred_element_type=jnp.float32,
    )
    coeffs = jnp.stack([prods[:, 0, 0] - prods[:, 1, 1], prods[:, 1, 0] + prods[:, 0, 1]], axis=1)
    degrees = coeffs.shape[2]
    good = (1 - flags).astype(jnp.float32)
    offset = lax.axis_index("chan") * f_dev
    good_here = lax.dynamic_slice_in_dim(good, offset, f_dev)
    cov_rows = lax.dynamic_slice_in_dim(fg_cov, offset, f_dev, 0)
    rows = coeffs.reshape(-1, f_dev)

    def spread_cov(vec):
        return lax.dot_general(
            lax.all_gather(vec, "chan", axis=1, tiled=True),
            cov_rows,
            (((1,), (1,)), ((), ())),
            precision=lax.Precision.HIGHEST,
            preferred_element_type=jnp.float32,
        )

    def curv_sum(values):
        return lax.psum(jnp.sum(values, axis=1), "chan")

    def norm_sum(values):
        return lax.psum(jnp.sum(values, axis=1), "chan")

    result = conjugate_fill(rows, good_here, spread_cov, curv_sum, norm_sum).reshape(
        m_dev, 2, degrees, f_dev
    )
    return result


def solution(mesh):
    placed = (P("tm", "chan", None), P("tm", "chan", None, None, None), P(), P(), P())
    return jax.shard_map(
        per_device,
        mesh=mesh,
        in_specs=placed,
        out_specs=P("tm", None, None, "chan"),
        check_vma=False,
    )
```

profile of v0, /device:TPU:1, one launch (start us, length us, event | category | flops | bytes accessed | tf_op | source)
XLA Modules:
  0.0 1975.6 jit_solution(2381233454197458835)
XLA Ops:
  6.5 2.8 copy.25
  10.1 0.6 copy.26
  10.7 0.6 copy.27
  11.5 1.1 pad_maximum_fusion
  12.8 0.9 constant_dynamic-slice_fusion
  13.7 78.5 %reduce-scatter.2.cloned.1.call-done = f32[2,32,512]{2,1,0:T(8,128)} async-done(((f32[16,32,512]{2,1,0:T(8,128)}), f32[2,32,512]{2,1,0:T(8,128)}) %reduce-scatter.2.cloned.1.call-update) | async-done | bytes 131088 | tf_op jit(solution)/shard_map/reduce_scatter | solution.py:56
  92.3 0.9 convert_element_type.12
  93.2 3.9 convolution_bitcast_fusion
  97.7 54.9 %psum.21 = f32[256,1]{0,1:T(1,128)S(1)} all-reduce(f32[256,1]{0,1:T(1,128)S(1)} %broadcast_in_dim.7), channel_id=1, replica_groups=mesh['tm'=8,'chan'=32] {'chan'}, use_global_device_ids=true, to_apply=%region_2.3 | all-reduce | flops 256 | bytes 2048 | tf_op jit(solution)/shard_map/psum | solution.py:86
  152.6 1748.1 %while.17 = (s32[]{:T(128)}, f32[256,32]{0,1:T(8,128)S(1)}, f32[256,32]{0,1:T(8,128)S(1)}, f32[256,32]{0,1:T(8,128)S(1)}, f32[256,1]{0,1:T(1,128)S(1)}, /*index=...) while((s32[]{:T(128)}, f32[256,32]{0,1:T(8,128)S(1)}, f32[256,32]{0,1:T(8,128)S(1)}, ...), condition=%wide.region_8.9_spmd.clone, body=%wide.region_3.8_spmd.clone.sunk | while | flops 100779008 | bytes 4836751 | solution.py:29
  152.6 0.7 broadcast_multiply_fusion.4
  153.4 64.9 %all-gather.5.cloned.1.call-done = f32[256,1024]{0,1:T(8,128)} async-done(((f32[256,32]{0,1:T(8,128)}), f32[256,1024]{0,1:T(8,128)}) %all-gather.5.cloned.1.call-update) | async-done | bytes 1048592 | tf_op jit(solution)/shard_map/while/body/eval_jaxpr/all_gather | solution.py:75
  218.3 1.9 multiply_reduce_fusion.5
  220.2 52.6 %psum.26 = f32[256]{0:T(256)S(1)} all-reduce(f32[256]{0:T(256)S(1)} %get-tuple-element.150), channel_id=1, replica_groups=mesh['tm'=8,'chan'=32] {'chan'}, use_global_device_ids=true, to_apply=%region_5.5 | all-reduce | flops 256 | bytes 2048 | tf_op jit(solution)/shard_map/while/body/eval_jaxpr/psum | solution.py:83
  272.9 54.6 %psum.27 = f32[256,1]{0,1:T(1,128)S(1)} all-reduce(f32[256,1]{0,1:T(1,128)S(1)} %bitcast.53), channel_id=1, replica_groups=mesh['tm'=8,'chan'=32] {'chan'}, use_global_device_ids=true, to_apply=%region_7.7 | all-reduce | flops 256 | bytes 2048 | tf_op jit(solution)/shard_map/while/body/eval_jaxpr/psum | solution.py:86
  327.6 0.7 broadcast_multiply_fusion.4
  328.3 64.9 %all-gather.5.cloned.1.call-done = f32[256,1024]{0,1:T(8,128)} async-done(((f32[256,32]{0,1:T(8,128)}), f32[256,1024]{0,1:T(8,128)}) %all-gather.5.cloned.1.call-update) | async-done | bytes 1048592 | tf_op jit(solution)/shard_map/while/body/eval_jaxpr/all_gather | solution.py:75
  393.2 1.9 multiply_reduce_fusion.5
  395.1 52.6 %psum.26 = f32[256]{0:T(256)S(1)} all-reduce(f32[256]{0:T(256)S(1)} %get-tuple-element.150), channel_id=1, replica_groups=mesh['tm'=8,'chan'=32] {'chan'}, use_global_device_ids=true, to_apply=%region_5.5 | all-reduce | flops 256 | bytes 2048 | tf_op jit(solution)/shard_map/while/body/eval_jaxpr/psum | solution.py:83
  447.8 54.6 %psum.27 = f32[256,1]{0,1:T(1,128)S(1)} all-reduce(f32[256,1]{0,1:T(1,128)S(1)} %bitcast.53), channel_id=1, replica_groups=mesh['tm'=8,'chan'=32] {'chan'}, use_global_device_ids=true, to_apply=%region_7.7 | all-reduce | flops 256 | bytes 2048 | tf_op jit(solution)/shard_map/while/body/eval_jaxpr/psum | solution.py:86
  502.5 0.7 broadcast_multiply_fusion.4
  503.2 64.6 %all-gather.5.cloned.1.call-done = f32[256,1024]{0,1:T(8,128)} async-done(((f32[256,32]{0,1:T(8,128)}), f32[256,1024]{0,1:T(8,128)}) %all-gather.5.cloned.1.call-update) | async-done | bytes 1048592 | tf_op jit(solution)/shard_map/while/body/eval_jaxpr/all_gather | solution.py:75
  567.9 1.9 multiply_reduce_fusion.5
  569.7 52.6 %psum.26 = f32[256]{0:T(256)S(1)} all-reduce(f32[256]{0:T(256)S(1)} %get-tuple-element.150), channel_id=1, replica_groups=mesh['tm'=8,'chan'=32] {'chan'}, use_global_device_ids=true, to_apply=%region_5.5 | all-reduce | flops 256 | bytes 2048 | tf_op jit(solution)/shard_map/while/body/eval_jaxpr/psum | solution.py:83
  622.4 54.6 %psum.27 = f32[256,1]{0,1:T(1,128)S(1)} all-reduce(f32[256,1]{0,1:T(1,128)S(1)} %bitcast.53), channel_id=1, replica_groups=mesh['tm'=8,'chan'=32] {'chan'}, use_global_device_ids=true, to_apply=%region_7.7 | all-reduce | flops 256 | bytes 2048 | tf_op jit(solution)/shard_map/while/body/eval_jaxpr/psum | solution.py:86
  677.1 0.7 broadcast_multiply_fusion.4
  677.9 64.6 %all-gather.5.cloned.1.call-done = f32[256,1024]{0,1:T(8,128)} async-done(((f32[256,32]{0,1:T(8,128)}), f32[256,1024]{0,1:T(8,128)}) %all-gather.5.cloned.1.call-update) | async-done | bytes 1048592 | tf_op jit(solution)/shard_map/while/body/eval_jaxpr/all_gather | solution.py:75
  742.5 1.9 multiply_reduce_fusion.5
  744.4 52.6 %psum.26 = f32[256]{0:T(256)S(1)} all-reduce(f32[256]{0:T(256)S(1)} %get-tuple-element.150), channel_id=1, replica_groups=mesh['tm'=8,'chan'=32] {'chan'}, use_global_device_ids=true, to_apply=%region_5.5 | all-reduce | flops 256 | bytes 2048 | tf_op jit(solution)/shard_map/while/body/eval_jaxpr/psum | solution.py:83
  797.1 54.6 %psum.27 = f32[256,1]{0,1:T(1,128)S(1)} all-reduce(f32[256,1]{0,1:T(1,128)S(1)} %bitcast.53), channel_id=1, replica_groups=mesh['tm'=8,'chan'=32] {'chan'}, use_global_device_ids=true, to_apply=%region_7.7 | all-reduce | flops 256 | bytes 2048 | tf_op jit(solution)/shard_map/while/body/eval_jaxpr/psum | solution.py:86
  851.8 0.7 broadcast_multiply_fusion.4
  852.5 64.6 %all-gather.5.cloned.1.call-done = f32[256,1024]{0,1:T(8,128)} async-done(((f32[256,32]{0,1:T(8,128)}), f32[256,1024]{0,1:T(8,128)}) %all-gather.5.cloned.1.call-update) | async-done | bytes 1048592 | tf_op jit(solution)/shard_map/while/body/eval_jaxpr/all_gather | solution.py:75
  917.1 1.9 multiply_reduce_fusion.5
  919.0 52.6 %psum.26 = f32[256]{0:T(256)S(1)} all-reduce(f32[256]{0:T(256)S(1)} %get-tuple-element.150), channel_id=1, replica_groups=mesh['tm'=8,'chan'=32] {'chan'}, use_global_device_ids=true, to_apply=%region_5.5 | all-reduce | flops 256 | bytes 2048 | tf_op jit(solution)/shard_map/while/body/eval_jaxpr/psum | solution.py:83
  971.7 54.6 %psum.27 = f32[256,1]{0,1:T(1,128)S(1)} all-reduce(f32[256,1]{0,1:T(1,128)S(1)} %bitcast.53), channel_id=1, replica_groups=mesh['tm'=8,'chan'=32] {'chan'}, use_global_device_ids=true, to_apply=%region_7.7 | all-reduce | flops 256 | bytes 2048 | tf_op jit(solution)/shard_map/while/body/eval_jaxpr/psum | solution.py:86
  1026.4 0.7 broadcast_multiply_fusion.4
  1027.1 65.0 %all-gather.5.cloned.1.call-done = f32[256,1024]{0,1:T(8,128)} async-done(((f32[256,32]{0,1:T(8,128)}), f32[256,1024]{0,1:T(8,128)}) %all-gather.5.cloned.1.call-update) | async-done | bytes 1048592 | tf_op jit(solution)/shard_map/while/body/eval_jaxpr/all_gather | solution.py:75
  1092.1 1.9 multiply_reduce_fusion.5
  1094.0 52.6 %psum.26 = f32[256]{0:T(256)S(1)} all-reduce(f32[256]{0:T(256)S(1)} %get-tuple-element.150), channel_id=1, replica_groups=mesh['tm'=8,'chan'=32] {'chan'}, use_global_device_ids=true, to_apply=%region_5.5 | all-reduce | flops 256 | bytes 2048 | tf_op jit(solution)/shard_map/while/body/eval_jaxpr/psum | solution.py:83
  1146.6 54.6 %psum.27 = f32[256,1]{0,1:T(1,128)S(1)} all-reduce(f32[256,1]{0,1:T(1,128)S(1)} %bitcast.53), channel_id=1, replica_groups=mesh['tm'=8,'chan'=32] {'chan'}, use_global_device_ids=true, to_apply=%region_7.7 | all-reduce | flops 256 | bytes 2048 | tf_op jit(solution)/shard_map/while/body/eval_jaxpr/psum | solution.py:86
  1201.3 0.7 broadcast_multiply_fusion.4
  1202.1 65.0 %all-gather.5.cloned.1.call-done = f32[256,1024]{0,1:T(8,128)} async-done(((f32[256,32]{0,1:T(8,128)}), f32[256,1024]{0,1:T(8,128)}) %all-gather.5.cloned.1.call-update) | async-done | bytes 1048592 | tf_op jit(solution)/shard_map/while/body/eval_jaxpr/all_gather | solution.py:75
  1267.0 1.9 multiply_reduce_fusion.5
  1268.9 52.6 %psum.26 = f32[256]{0:T(256)S(1)} all-reduce(f32[256]{0:T(256)S(1)} %get-tuple-element.150), channel_id=1, replica_groups=mesh['tm'=8,'chan'=32] {'chan'}, use_global_device_ids=true, to_apply=%region_5.5 | all-reduce | flops 256 | bytes 2048 | tf_op jit(solution)/shard_map/while/body/eval_jaxpr/psum | solution.py:83
  1321.6 54.6 %psum.27 = f32[256,1]{0,1:T(1,128)S(1)} all-reduce(f32[256,1]{0,1:T(1,128)S(1)} %bitcast.53), channel_id=1, replica_groups=mesh['tm'=8,'chan'=32] {'chan'}, use_global_device_ids=true, to_apply=%region_7.7 | all-reduce | flops 256 | bytes 2048 | tf_op jit(solution)/shard_map/while/body/eval_jaxpr/psum | solution.py:86
  1376.3 0.7 broadcast_multiply_fusion.4
  1377.0 64.9 %all-gather.5.cloned.1.call-done = f32[256,1024]{0,1:T(8,128)} async-done(((f32[256,32]{0,1:T(8,128)}), f32[256,1024]{0,1:T(8,128)}) %all-gather.5.cloned.1.call-update) | async-done | bytes 1048592 | tf_op jit(solution)/shard_map/while/body/eval_jaxpr/all_gather | solution.py:75
  1442.0 1.9 multiply_reduce_fusion.5
  1443.9 52.6 %psum.26 = f32[256]{0:T(256)S(1)} all-reduce(f32[256]{0:T(256)S(1)} %get-tuple-element.150), channel_id=1, replica_groups=mesh['tm'=8,'chan'=32] {'chan'}, use_global_device_ids=true, to_apply=%region_5.5 | all-reduce | flops 256 | bytes 2048 | tf_op jit(solution)/shard_map/while/body/eval_jaxpr/psum | solution.py:83
  1496.5 54.6 %psum.27 = f32[256,1]{0,1:T(1,128)S(1)} all-reduce(f32[256,1]{0,1:T(1,128)S(1)} %bitcast.53), channel_id=1, replica_groups=mesh['tm'=8,'chan'=32] {'chan'}, use_global_device_ids=true, to_apply=%region_7.7 | all-reduce | flops 256 | bytes 2048 | tf_op jit(solution)/shard_map/while/body/eval_jaxpr/psum | solution.py:86
  1551.2 0.7 broadcast_multiply_fusion.4
  1552.0 64.6 %all-gather.5.cloned.1.call-done = f32[256,1024]{0,1:T(8,128)} async-done(((f32[256,32]{0,1:T(8,128)}), f32[256,1024]{0,1:T(8,128)}) %all-gather.5.cloned.1.call-update) | async-done | bytes 1048592 | tf_op jit(solution)/shard_map/while/body/eval_jaxpr/all_gather | solution.py:75
  1616.6 1.9 multiply_reduce_fusion.5
  1618.5 52.6 %psum.26 = f32[256]{0:T(256)S(1)} all-reduce(f32[256]{0:T(256)S(1)} %get-tuple-element.150), channel_id=1, replica_groups=mesh['tm'=8,'chan'=32] {'chan'}, use_global_device_ids=true, to_apply=%region_5.5 | all-reduce | flops 256 | bytes 2048 | tf_op jit(solution)/shard_map/while/body/eval_jaxpr/psum | solution.py:83
  1671.2 54.6 %psum.27 = f32[256,1]{0,1:T(1,128)S(1)} all-reduce(f32[256,1]{0,1:T(1,128)S(1)} %bitcast.53), channel_id=1, replica_groups=mesh['tm'=8,'chan'=32] {'chan'}, use_global_device_ids=true, to_apply=%region_7.7 | all-reduce | flops 256 | bytes 2048 | tf_op jit(solution)/shard_map/while/body/eval_jaxpr/psum | solution.py:86
  1725.9 0.7 broadcast_multiply_fusion.4
  1726.6 64.9 %all-gather.5.cloned.1.call-done = f32[256,1024]{0,1:T(8,128)} async-done(((f32[256,32]{0,1:T(8,128)}), f32[256,1024]{0,1:T(8,128)}) %all-gather.5.cloned.1.call-update) | async-done | bytes 1048592 | tf_op jit(solution)/shard_map/while/body/eval_jaxpr/all_gather | solution.py:75
  1791.5 1.9 multiply_reduce_fusion.5
  1793.4 52.6 %psum.26 = f32[256]{0:T(256)S(1)} all-reduce(f32[256]{0:T(256)S(1)} %get-tuple-element.150), channel_id=1, replica_groups=mesh['tm'=8,'chan'=32] {'chan'}, use_global_device_ids=true, to_apply=%region_5.5 | all-reduce | flops 256 | bytes 2048 | tf_op jit(solution)/shard_map/while/body/eval_jaxpr/psum | solution.py:83
  1846.1 54.6 %psum.27 = f32[256,1]{0,1:T(1,128)S(1)} all-reduce(f32[256,1]{0,1:T(1,128)S(1)} %bitcast.53), channel_id=1, replica_groups=mesh['tm'=8,'chan'=32] {'chan'}, use_global_device_ids=true, to_apply=%region_7.7 | all-reduce | flops 256 | bytes 2048 | tf_op jit(solution)/shard_map/while/body/eval_jaxpr/psum | solution.py:86
  1900.8 0.7 broadcast_multiply_fusion.1
  1901.5 64.6 %all-gather.3.cloned.1.call-done = f32[256,1024]{0,1:T(8,128)} async-done(((f32[256,32]{0,1:T(8,128)}), f32[256,1024]{0,1:T(8,128)}) %all-gather.3.cloned.1.call-update) | async-done | bytes 1048592 | tf_op jit(solution)/shard_map/all_gather | solution.py:75
  1966.2 1.9 fusion.1
  1968.2 0.6 copy.21
  (108 shorter events, 3.0 us)
Async XLA Ops:
  6.5 85.7 %reduce-scatter.2.cloned.1.call-start = ((), (), s32[]{:S(2)}) async-start(), calls=%async_computation.1 | async-start | bytes 1179648 | tf_op jit(solution)/shard_map/reduce_scatter | solution.py:56
  6.5 2.9 copy-start.1
  11.5 1.2 copy-start
  152.6 65.7 %all-gather.5.cloned.1.call-start = ((), (), s32[]{:S(2)}) async-start(), calls=%async_computation.3 | async-start | bytes 1081344 | tf_op jit(solution)/shard_map/while/body/eval_jaxpr/all_gather | solution.py:75
  327.5 65.7 %all-gather.5.cloned.1.call-start = ((), (), s32[]{:S(2)}) async-start(), calls=%async_computation.3 | async-start | bytes 1081344 | tf_op jit(solution)/shard_map/while/body/eval_jaxpr/all_gather | solution.py:75
  502.5 65.4 %all-gather.5.cloned.1.call-start = ((), (), s32[]{:S(2)}) async-start(), calls=%async_computation.3 | async-start | bytes 1081344 | tf_op jit(solution)/shard_map/while/body/eval_jaxpr/all_gather | solution.py:75
  677.1 65.4 %all-gather.5.cloned.1.call-start = ((), (), s32[]{:S(2)}) async-start(), calls=%async_computation.3 | async-start | bytes 1081344 | tf_op jit(solution)/shard_map/while/body/eval_jaxpr/all_gather | solution.py:75
  851.7 65.4 %all-gather.5.cloned.1.call-start = ((), (), s32[]{:S(2)}) async-start(), calls=%async_computation.3 | async-start | bytes 1081344 | tf_op jit(solution)/shard_map/while/body/eval_jaxpr/all_gather | solution.py:75
  1026.4 65.7 %all-gather.5.cloned.1.call-start = ((), (), s32[]{:S(2)}) async-start(), calls=%async_computation.3 | async-start | bytes 1081344 | tf_op jit(solution)/shard_map/while/body/eval_jaxpr/all_gather | solution.py:75
  1201.3 65.7 %all-gather.5.cloned.1.call-start = ((), (), s32[]{:S(2)}) async-start(), calls=%async_computation.3 | async-start | bytes 1081344 | tf_op jit(solution)/shard_map/while/body/eval_jaxpr/all_gather | solution.py:75
  1376.2 65.7 %all-gather.5.cloned.1.call-start = ((), (), s32[]{:S(2)}) async-start(), calls=%async_computation.3 | async-start | bytes 1081344 | tf_op jit(solution)/shard_map/while/body/eval_jaxpr/all_gather | solution.py:75
  1551.2 65.4 %all-gather.5.cloned.1.call-start = ((), (), s32[]{:S(2)}) async-start(), calls=%async_computation.3 | async-start | bytes 1081344 | tf_op jit(solution)/shard_map/while/body/eval_jaxpr/all_gather | solution.py:75
  1725.8 65.7 %all-gather.5.cloned.1.call-start = ((), (), s32[]{:S(2)}) async-start(), calls=%async_computation.3 | async-start | bytes 1081344 | tf_op jit(solution)/shard_map/while/body/eval_jaxpr/all_gather | solution.py:75
  1900.8 65.4 %all-gather.3.cloned.1.call-start = ((), (), s32[]{:S(2)}) async-start(), calls=%async_computation.2 | async-start | bytes 1081344 | tf_op jit(solution)/shard_map/all_gather | solution.py:75
Sparse Core Ops, SparseCore 0:
  12.8 79.3 reduce-scatter.1
  155.3 62.9 all-gather.4
  330.2 63.0 all-gather.4
  504.8 63.0 all-gather.4
  679.4 63.0 all-gather.4
  854.1 63.0 all-gather.4
  1029.0 63.0 all-gather.4
  1204.0 63.0 all-gather.4
  1378.9 63.0 all-gather.4
  1553.6 63.0 all-gather.4
  1728.5 62.9 all-gather.4
  1903.1 63.0 all-gather.2
where the time goes:
time: 1980 us
  blocking collectives  1130 us (57%)
  waiting for transfers between devices  792 us (40%)
  matrix products  25.1 us (1%)
    all_gather x11, waiting for transfers between devices, spread_cov(): lax.all_gather(vec, 'chan', axis=1, tiled=True)  713 us
    psum x11, blocking collectives, norm_sum(): return lax.psum(jnp.sum(values, axis=1), 'chan')  601 us
    psum x10, blocking collectives, curv_sum(): return lax.psum(jnp.sum(values, axis=1), 'chan')  526 us
    reduce_scatter x1, waiting for transfers between devices, per_device(): lax.psum_scatter(jnp.concatenate([real_part, imag_part], axis=-1), 'tm',...  78.5 us
  transfers between devices with their start and end apart: 12, of which 12 were waited for; matrix products, arithmetic and copies ran while one was open for 0% of the time, Pallas kernels for 0%

commit v1 on v0

--- a/solution.py
+++ b/solution.py
@@ -72,7 +72,9 @@
 
     def spread_cov(vec):
         return lax.dot_general(
-            lax.all_gather(vec, "chan", axis=1, tiled=True),
+            jnp.concatenate(
+                lax.all_to_all(jnp.stack([vec] * lax.axis_size("chan")), "chan", 0, 0), axis=1
+            ),
             cov_rows,
             (((1,), (1,)), ((), ())),
             precision=lax.Precision.HIGHEST,

time: 1980 us -> 1620 us (0.82)
  waiting for transfers between devices: 792 us -> 359 us
  starting transfers between devices: 0.45 us -> 61.7 us
  blocking collectives: 1130 us -> 1150 us
    all_gather x11 -> x0, waiting for transfers between devices: 713 us -> none  [spread_cov(): lax.all_gather(vec, 'chan', axis=1, tiled=True)]
    all_to_all x0 -> x10, waiting for transfers between devices: none -> 281 us  [spread_cov(): lax.all_to_all(jnp.stack([vec] * lax.axis_size('chan')), 'chan', 0, 0)]
    all_to_all x0 -> x10, starting transfers between devices: none -> 61.7 us  [spread_cov(): lax.all_to_all(jnp.stack([vec] * lax.axis_size('chan')), 'chan', 0, 0)]
    all_to_all x0 -> x1, blocking collectives: none -> 33.9 us  [spread_cov(): lax.all_to_all(jnp.stack([vec] * lax.axis_size('chan')), 'chan', 0, 0)]
  transfers between devices with their start and end apart: 12 -> 11, of which waited for: 12 -> 11; matrix products, arithmetic and copies ran while one was open for 0% -> 0% of each run, Pallas kernels for 0% -> 0%
where the time goes in v1:
time: 1620 us
  blocking collectives  1150 us (71%)
  waiting for transfers between devices  359 us (22%)
  starting transfers between devices  61.7 us (4%)
  local copies, waits for them, and re-layouts  17.4 us (1%)
    psum x11, blocking collectives, norm_sum(): return lax.psum(jnp.sum(values, axis=1), 'chan')  585 us
    psum x10, blocking collectives, curv_sum(): return lax.psum(jnp.sum(values, axis=1), 'chan')  531 us
    all_to_all x10, waiting for transfers between devices, spread_cov(): lax.all_to_all(jnp.stack([vec] * lax.axis_size('chan')), 'chan', 0, 0)  281 us
    reduce_scatter x1, waiting for transfers between devices, per_device(): lax.psum_scatter(jnp.concatenate([real_part, imag_part], axis=-1), 'tm',...  78.6 us
    all_to_all x10, starting transfers between devices, spread_cov(): lax.all_to_all(jnp.stack([vec] * lax.axis_size('chan')), 'chan', 0, 0)  61.7 us
    all_to_all x1, blocking collectives, spread_cov(): lax.all_to_all(jnp.stack([vec] * lax.axis_size('chan')), 'chan', 0, 0)  33.9 us
  transfers between devices with their start and end apart: 11, of which 11 were waited for; matrix products, arithmetic and copies ran while one was open for 0% of the time, Pallas kernels for 0%

profile of v1, /device:TPU:1, one launch (start us, length us, event | category | flops | bytes accessed | tf_op | source)
XLA Modules:
  0.0 1617.8 jit_solution(14337200872379805944)
XLA Ops:
  6.5 2.8 copy.27
  11.5 1.1 pad_maximum_fusion
  12.8 0.9 constant_dynamic-slice_fusion
  13.7 78.6 %reduce-scatter.2.cloned.1.call-done = f32[2,32,512]{2,1,0:T(8,128)} async-done(((f32[16,32,512]{2,1,0:T(8,128)}), f32[2,32,512]{2,1,0:T(8,128)}) %reduce-scatter.2.cloned.1.call-update) | async-done | bytes 131088 | tf_op jit(solution)/shard_map/reduce_scatter | solution.py:56
  92.3 0.9 convert_element_type.12
  93.2 3.9 convolution_bitcast_fusion
  97.7 54.9 %psum.21 = f32[256,1]{0,1:T(1,128)S(1)} all-reduce(f32[256,1]{0,1:T(1,128)S(1)} %broadcast_in_dim.7), channel_id=1, replica_groups=mesh['tm'=8,'chan'=32] {'chan'}, use_global_device_ids=true, to_apply=%region_2.3 | all-reduce | flops 256 | bytes 2048 | tf_op jit(solution)/shard_map/psum | solution.py:88
  152.6 1422.9 %while.17 = (s32[]{:T(128)}, f32[256,32]{0,1:T(8,128)S(1)}, f32[256,32]{0,1:T(8,128)S(1)}, f32[256,32]{0,1:T(8,128)S(1)}, f32[256,1]{0,1:T(1,128)S(1)}, /*index=...) while((s32[]{:T(128)}, f32[256,32]{0,1:T(8,128)S(1)}, f32[256,32]{0,1:T(8,128)S(1)}, ...), condition=%wide.region_8.9_spmd.clone, body=%wide.region_3.8_spmd.clone.sunk | while | flops 100779008 | bytes 5819783 | solution.py:29
  152.7 1.1 stack.10
  153.8 7.8 all-to-all-start
  161.6 28.1 %all-to-all-done = f32[32,256,32]{1,2,0:T(8,128)S(1)} async-done(((f32[32,256,32]{1,2,0:T(8,128)}), f32[32,256,32]{1,2,0:T(8,128)S(1)}, u32[]{:S(2)}, u32[]{:S(2)}) %all-to-all-start) | async-done | bytes 1048608 | tf_op jit(solution)/shard_map/while/body/eval_jaxpr/all_to_all | solution.py:76
  189.7 0.7 multiply_reduce_fusion.5
  190.4 53.1 %psum.26 = f32[256]{0:T(256)S(1)} all-reduce(f32[256]{0:T(256)S(1)} %get-tuple-element.150), channel_id=1, replica_groups=mesh['tm'=8,'chan'=32] {'chan'}, use_global_device_ids=true, to_apply=%region_5.5 | all-reduce | flops 256 | bytes 2048 | tf_op jit(solution)/shard_map/while/body/eval_jaxpr/psum | solution.py:85
  243.5 53.0 %psum.27 = f32[256,1]{0,1:T(1,128)S(1)} all-reduce(f32[256,1]{0,1:T(1,128)S(1)} %bitcast.63), channel_id=1, replica_groups=mesh['tm'=8,'chan'=32] {'chan'}, use_global_device_ids=true, to_apply=%region_7.7 | all-reduce | flops 256 | bytes 2048 | tf_op jit(solution)/shard_map/while/body/eval_jaxpr/psum | solution.py:88
  296.6 1.1 stack.10
  297.8 6.0 all-to-all-start
  303.8 28.1 %all-to-all-done = f32[32,256,32]{1,2,0:T(8,128)S(1)} async-done(((f32[32,256,32]{1,2,0:T(8,128)}), f32[32,256,32]{1,2,0:T(8,128)S(1)}, u32[]{:S(2)}, u32[]{:S(2)}) %all-to-all-start) | async-done | bytes 1048608 | tf_op jit(solution)/shard_map/while/body/eval_jaxpr/all_to_all | solution.py:76
  332.5 53.1 %psum.26 = f32[256]{0:T(256)S(1)} all-reduce(f32[256]{0:T(256)S(1)} %get-tuple-element.150), channel_id=1, replica_groups=mesh['tm'=8,'chan'=32] {'chan'}, use_global_device_ids=true, to_apply=%region_5.5 | all-reduce | flops 256 | bytes 2048 | tf_op jit(solution)/shard_map/while/body/eval_jaxpr/psum | solution.py:85
  385.6 53.0 %psum.27 = f32[256,1]{0,1:T(1,128)S(1)} all-reduce(f32[256,1]{0,1:T(1,128)S(1)} %bitcast.63), channel_id=1, replica_groups=mesh['tm'=8,'chan'=32] {'chan'}, use_global_device_ids=true, to_apply=%region_7.7 | all-reduce | flops 256 | bytes 2048 | tf_op jit(solution)/shard_map/while/body/eval_jaxpr/psum | solution.py:88
  438.8 1.1 stack.10
  439.9 6.0 all-to-all-start
  445.9 28.1 %all-to-all-done = f32[32,256,32]{1,2,0:T(8,128)S(1)} async-done(((f32[32,256,32]{1,2,0:T(8,128)}), f32[32,256,32]{1,2,0:T(8,128)S(1)}, u32[]{:S(2)}, u32[]{:S(2)}) %all-to-all-start) | async-done | bytes 1048608 | tf_op jit(solution)/shard_map/while/body/eval_jaxpr/all_to_all | solution.py:76
  474.6 53.1 %psum.26 = f32[256]{0:T(256)S(1)} all-reduce(f32[256]{0:T(256)S(1)} %get-tuple-element.150), channel_id=1, replica_groups=mesh['tm'=8,'chan'=32] {'chan'}, use_global_device_ids=true, to_apply=%region_5.5 | all-reduce | flops 256 | bytes 2048 | tf_op jit(solution)/shard_map/while/body/eval_jaxpr/psum | solution.py:85
  527.7 53.0 %psum.27 = f32[256,1]{0,1:T(1,128)S(1)} all-reduce(f32[256,1]{0,1:T(1,128)S(1)} %bitcast.63), channel_id=1, replica_groups=mesh['tm'=8,'chan'=32] {'chan'}, use_global_device_ids=true, to_apply=%region_7.7 | all-reduce | flops 256 | bytes 2048 | tf_op jit(solution)/shard_map/while/body/eval_jaxpr/psum | solution.py:88
  580.9 1.1 stack.10
  582.0 6.0 all-to-all-start
  588.0 28.1 %all-to-all-done = f32[32,256,32]{1,2,0:T(8,128)S(1)} async-done(((f32[32,256,32]{1,2,0:T(8,128)}), f32[32,256,32]{1,2,0:T(8,128)S(1)}, u32[]{:S(2)}, u32[]{:S(2)}) %all-to-all-start) | async-done | bytes 1048608 | tf_op jit(solution)/shard_map/while/body/eval_jaxpr/all_to_all | solution.py:76
  616.0 0.7 multiply_reduce_fusion.5
  616.7 53.1 %psum.26 = f32[256]{0:T(256)S(1)} all-reduce(f32[256]{0:T(256)S(1)} %get-tuple-element.150), channel_id=1, replica_groups=mesh['tm'=8,'chan'=32] {'chan'}, use_global_device_ids=true, to_apply=%region_5.5 | all-reduce | flops 256 | bytes 2048 | tf_op jit(solution)/shard_map/while/body/eval_jaxpr/psum | solution.py:85
  669.9 53.0 %psum.27 = f32[256,1]{0,1:T(1,128)S(1)} all-reduce(f32[256,1]{0,1:T(1,128)S(1)} %bitcast.63), channel_id=1, replica_groups=mesh['tm'=8,'chan'=32] {'chan'}, use_global_device_ids=true, to_apply=%region_7.7 | all-reduce | flops 256 | bytes 2048 | tf_op jit(solution)/shard_map/while/body/eval_jaxpr/psum | solution.py:88
  723.0 1.1 stack.10
  724.1 6.0 all-to-all-start
  730.1 28.1 %all-to-all-done = f32[32,256,32]{1,2,0:T(8,128)S(1)} async-done(((f32[32,256,32]{1,2,0:T(8,128)}), f32[32,256,32]{1,2,0:T(8,128)S(1)}, u32[]{:S(2)}, u32[]{:S(2)}) %all-to-all-start) | async-done | bytes 1048608 | tf_op jit(solution)/shard_map/while/body/eval_jaxpr/all_to_all | solution.py:76
  758.2 0.7 multiply_reduce_fusion.5
  758.8 53.1 %psum.26 = f32[256]{0:T(256)S(1)} all-reduce(f32[256]{0:T(256)S(1)} %get-tuple-element.150), channel_id=1, replica_groups=mesh['tm'=8,'chan'=32] {'chan'}, use_global_device_ids=true, to_apply=%region_5.5 | all-reduce | flops 256 | bytes 2048 | tf_op jit(solution)/shard_map/while/body/eval_jaxpr/psum | solution.py:85
  812.0 53.0 %psum.27 = f32[256,1]{0,1:T(1,128)S(1)} all-reduce(f32[256,1]{0,1:T(1,128)S(1)} %bitcast.63), channel_id=1, replica_groups=mesh['tm'=8,'chan'=32] {'chan'}, use_global_device_ids=true, to_apply=%region_7.7 | all-reduce | flops 256 | bytes 2048 | tf_op jit(solution)/shard_map/while/body/eval_jaxpr/psum | solution.py:88
  865.1 1.1 stack.10
  866.2 6.0 all-to-all-start
  872.2 28.1 %all-to-all-done = f32[32,256,32]{1,2,0:T(8,128)S(1)} async-done(((f32[32,256,32]{1,2,0:T(8,128)}), f32[32,256,32]{1,2,0:T(8,128)S(1)}, u32[]{:S(2)}, u32[]{:S(2)}) %all-to-all-start) | async-done | bytes 1048608 | tf_op jit(solution)/shard_map/while/body/eval_jaxpr/all_to_all | solution.py:76
  900.3 0.7 multiply_reduce_fusion.5
  900.9 53.1 %psum.26 = f32[256]{0:T(256)S(1)} all-reduce(f32[256]{0:T(256)S(1)} %get-tuple-element.150), channel_id=1, replica_groups=mesh['tm'=8,'chan'=32] {'chan'}, use_global_device_ids=true, to_apply=%region_5.5 | all-reduce | flops 256 | bytes 2048 | tf_op jit(solution)/shard_map/while/body/eval_jaxpr/psum | solution.py:85
  954.1 53.0 %psum.27 = f32[256,1]{0,1:T(1,128)S(1)} all-reduce(f32[256,1]{0,1:T(1,128)S(1)} %bitcast.63), channel_id=1, replica_groups=mesh['tm'=8,'chan'=32] {'chan'}, use_global_device_ids=true, to_apply=%region_7.7 | all-reduce | flops 256 | bytes 2048 | tf_op jit(solution)/shard_map/while/body/eval_jaxpr/psum | solution.py:88
  1007.2 1.1 stack.10
  1008.3 6.0 all-to-all-start
  1014.3 28.1 %all-to-all-done = f32[32,256,32]{1,2,0:T(8,128)S(1)} async-done(((f32[32,256,32]{1,2,0:T(8,128)}), f32[32,256,32]{1,2,0:T(8,128)S(1)}, u32[]{:S(2)}, u32[]{:S(2)}) %all-to-all-start) | async-done | bytes 1048608 | tf_op jit(solution)/shard_map/while/body/eval_jaxpr/all_to_all | solution.py:76
  1043.0 53.1 %psum.26 = f32[256]{0:T(256)S(1)} all-reduce(f32[256]{0:T(256)S(1)} %get-tuple-element.150), channel_id=1, replica_groups=mesh['tm'=8,'chan'=32] {'chan'}, use_global_device_ids=true, to_apply=%region_5.5 | all-reduce | flops 256 | bytes 2048 | tf_op jit(solution)/shard_map/while/body/eval_jaxpr/psum | solution.py:85
  1096.2 53.0 %psum.27 = f32[256,1]{0,1:T(1,128)S(1)} all-reduce(f32[256,1]{0,1:T(1,128)S(1)} %bitcast.63), channel_id=1, replica_groups=mesh['tm'=8,'chan'=32] {'chan'}, use_global_device_ids=true, to_apply=%region_7.7 | all-reduce | flops 256 | bytes 2048 | tf_op jit(solution)/shard_map/while/body/eval_jaxpr/psum | solution.py:88
  1149.3 1.1 stack.10
  1150.4 6.0 all-to-all-start
  1156.4 28.1 %all-to-all-done = f32[32,256,32]{1,2,0:T(8,128)S(1)} async-done(((f32[32,256,32]{1,2,0:T(8,128)}), f32[32,256,32]{1,2,0:T(8,128)S(1)}, u32[]{:S(2)}, u32[]{:S(2)}) %all-to-all-start) | async-done | bytes 1048608 | tf_op jit(solution)/shard_map/while/body/eval_jaxpr/all_to_all | solution.py:76
  1185.2 53.1 %psum.26 = f32[256]{0:T(256)S(1)} all-reduce(f32[256]{0:T(256)S(1)} %get-tuple-element.150), channel_id=1, replica_groups=mesh['tm'=8,'chan'=32] {'chan'}, use_global_device_ids=true, to_apply=%region_5.5 | all-reduce | flops 256 | bytes 2048 | tf_op jit(solution)/shard_map/while/body/eval_jaxpr/psum | solution.py:85
  1238.3 53.0 %psum.27 = f32[256,1]{0,1:T(1,128)S(1)} all-reduce(f32[256,1]{0,1:T(1,128)S(1)} %bitcast.63), channel_id=1, replica_groups=mesh['tm'=8,'chan'=32] {'chan'}, use_global_device_ids=true, to_apply=%region_7.7 | all-reduce | flops 256 | bytes 2048 | tf_op jit(solution)/shard_map/while/body/eval_jaxpr/psum | solution.py:88
  1291.4 1.1 stack.10
  1292.5 6.0 all-to-all-start
  1298.5 28.1 %all-to-all-done = f32[32,256,32]{1,2,0:T(8,128)S(1)} async-done(((f32[32,256,32]{1,2,0:T(8,128)}), f32[32,256,32]{1,2,0:T(8,128)S(1)}, u32[]{:S(2)}, u32[]{:S(2)}) %all-to-all-start) | async-done | bytes 1048608 | tf_op jit(solution)/shard_map/while/body/eval_jaxpr/all_to_all | solution.py:76
  1326.6 0.7 multiply_reduce_fusion.5
  1327.3 53.1 %psum.26 = f32[256]{0:T(256)S(1)} all-reduce(f32[256]{0:T(256)S(1)} %get-tuple-element.150), channel_id=1, replica_groups=mesh['tm'=8,'chan'=32] {'chan'}, use_global_device_ids=true, to_apply=%region_5.5 | all-reduce | flops 256 | bytes 2048 | tf_op jit(solution)/shard_map/while/body/eval_jaxpr/psum | solution.py:85
  1380.4 53.0 %psum.27 = f32[256,1]{0,1:T(1,128)S(1)} all-reduce(f32[256,1]{0,1:T(1,128)S(1)} %bitcast.63), channel_id=1, replica_groups=mesh['tm'=8,'chan'=32] {'chan'}, use_global_device_ids=true, to_apply=%region_7.7 | all-reduce | flops 256 | bytes 2048 | tf_op jit(solution)/shard_map/while/body/eval_jaxpr/psum | solution.py:88
  1433.5 1.1 stack.10
  1434.6 6.0 all-to-all-start
  1440.6 28.1 %all-to-all-done = f32[32,256,32]{1,2,0:T(8,128)S(1)} async-done(((f32[32,256,32]{1,2,0:T(8,128)}), f32[32,256,32]{1,2,0:T(8,128)S(1)}, u32[]{:S(2)}, u32[]{:S(2)}) %all-to-all-start) | async-done | bytes 1048608 | tf_op jit(solution)/shard_map/while/body/eval_jaxpr/all_to_all | solution.py:76
  1469.4 53.1 %psum.26 = f32[256]{0:T(256)S(1)} all-reduce(f32[256]{0:T(256)S(1)} %get-tuple-element.150), channel_id=1, replica_groups=mesh['tm'=8,'chan'=32] {'chan'}, use_global_device_ids=true, to_apply=%region_5.5 | all-reduce | flops 256 | bytes 2048 | tf_op jit(solution)/shard_map/while/body/eval_jaxpr/psum | solution.py:85
  1522.5 53.0 %psum.27 = f32[256,1]{0,1:T(1,128)S(1)} all-reduce(f32[256,1]{0,1:T(1,128)S(1)} %bitcast.63), channel_id=1, replica_groups=mesh['tm'=8,'chan'=32] {'chan'}, use_global_device_ids=true, to_apply=%region_7.7 | all-reduce | flops 256 | bytes 2048 | tf_op jit(solution)/shard_map/while/body/eval_jaxpr/psum | solution.py:88
  1575.7 33.9 %all_to_all.12 = f32[32,256,32]{1,2,0:T(8,128)S(1)} all-to-all(f32[32,256,32]{1,2,0:T(8,128)S(1)} %stack.7), channel_id=1, replica_groups=mesh['tm'=8,'chan'=32] {'chan'}, dimensions={0} | all-to-all | bytes 2097152 | tf_op jit(solution)/shard_map/all_to_all | solution.py:76
  (107 shorter events, 9.2 us)
Async XLA Ops:
  6.5 85.7 %reduce-scatter.2.cloned.1.call-start = ((), (), s32[]{:S(2)}) async-start(), calls=%async_computation.3 | async-start | bytes 1179648 | tf_op jit(solution)/shard_map/reduce_scatter | solution.py:56
  6.5 2.9 copy-start.1
  11.5 1.2 copy-start
  153.8 35.9 %all-to-all-start = ((f32[32,256,32]{1,2,0:T(8,128)}), f32[32,256,32]{1,2,0:T(8,128)S(1)}, u32[]{:S(2)}, u32[]{:S(2)}) async-start(f32[32,256,32]{1,2,0:T(8,128)} %stack.10), calls=%async_computation | async-start | bytes 2097152 | tf_op jit(solution)/shard_map/while/body/eval_jaxpr/all_to_all | solution.py:76
  297.8 34.1 %all-to-all-start = ((f32[32,256,32]{1,2,0:T(8,128)}), f32[32,256,32]{1,2,0:T(8,128)S(1)}, u32[]{:S(2)}, u32[]{:S(2)}) async-start(f32[32,256,32]{1,2,0:T(8,128)} %stack.10), calls=%async_computation | async-start | bytes 2097152 | tf_op jit(solution)/shard_map/while/body/eval_jaxpr/all_to_all | solution.py:76
  439.9 34.1 %all-to-all-start = ((f32[32,256,32]{1,2,0:T(8,128)}), f32[32,256,32]{1,2,0:T(8,128)S(1)}, u32[]{:S(2)}, u32[]{:S(2)}) async-start(f32[32,256,32]{1,2,0:T(8,128)} %stack.10), calls=%async_computation | async-start | bytes 2097152 | tf_op jit(solution)/shard_map/while/body/eval_jaxpr/all_to_all | solution.py:76
  582.0 34.1 %all-to-all-start = ((f32[32,256,32]{1,2,0:T(8,128)}), f32[32,256,32]{1,2,0:T(8,128)S(1)}, u32[]{:S(2)}, u32[]{:S(2)}) async-start(f32[32,256,32]{1,2,0:T(8,128)} %stack.10), calls=%async_computation | async-start | bytes 2097152 | tf_op jit(solution)/shard_map/while/body/eval_jaxpr/all_to_all | solution.py:76
  724.1 34.1 %all-to-all-start = ((f32[32,256,32]{1,2,0:T(8,128)}), f32[32,256,32]{1,2,0:T(8,128)S(1)}, u32[]{:S(2)}, u32[]{:S(2)}) async-start(f32[32,256,32]{1,2,0:T(8,128)} %stack.10), calls=%async_computation | async-start | bytes 2097152 | tf_op jit(solution)/shard_map/while/body/eval_jaxpr/all_to_all | solution.py:76
  866.2 34.1 %all-to-all-start = ((f32[32,256,32]{1,2,0:T(8,128)}), f32[32,256,32]{1,2,0:T(8,128)S(1)}, u32[]{:S(2)}, u32[]{:S(2)}) async-start(f32[32,256,32]{1,2,0:T(8,128)} %stack.10), calls=%async_computation | async-start | bytes 2097152 | tf_op jit(solution)/shard_map/while/body/eval_jaxpr/all_to_all | solution.py:76
  1008.3 34.1 %all-to-all-start = ((f32[32,256,32]{1,2,0:T(8,128)}), f32[32,256,32]{1,2,0:T(8,128)S(1)}, u32[]{:S(2)}, u32[]{:S(2)}) async-start(f32[32,256,32]{1,2,0:T(8,128)} %stack.10), calls=%async_computation | async-start | bytes 2097152 | tf_op jit(solution)/shard_map/while/body/eval_jaxpr/all_to_all | solution.py:76
  1150.4 34.1 %all-to-all-start = ((f32[32,256,32]{1,2,0:T(8,128)}), f32[32,256,32]{1,2,0:T(8,128)S(1)}, u32[]{:S(2)}, u32[]{:S(2)}) async-start(f32[32,256,32]{1,2,0:T(8,128)} %stack.10), calls=%async_computation | async-start | bytes 2097152 | tf_op jit(solution)/shard_map/while/body/eval_jaxpr/all_to_all | solution.py:76
  1292.5 34.1 %all-to-all-start = ((f32[32,256,32]{1,2,0:T(8,128)}), f32[32,256,32]{1,2,0:T(8,128)S(1)}, u32[]{:S(2)}, u32[]{:S(2)}) async-start(f32[32,256,32]{1,2,0:T(8,128)} %stack.10), calls=%async_computation | async-start | bytes 2097152 | tf_op jit(solution)/shard_map/while/body/eval_jaxpr/all_to_all | solution.py:76
  1434.6 34.1 %all-to-all-start = ((f32[32,256,32]{1,2,0:T(8,128)}), f32[32,256,32]{1,2,0:T(8,128)S(1)}, u32[]{:S(2)}, u32[]{:S(2)}) async-start(f32[32,256,32]{1,2,0:T(8,128)} %stack.10), calls=%async_computation | async-start | bytes 2097152 | tf_op jit(solution)/shard_map/while/body/eval_jaxpr/all_to_all | solution.py:76
Sparse Core Ops, SparseCore 0:
  12.8 79.4 reduce-scatter.1
